TPU v7x, 32 devices: a whole 2x2x4 slice. The times are simulated.
32 devices in a mesh: slab: 4 (over y, x), leaf: 8 (over z, core).
Axes of the slice: x: 2, y: 2, z: 4, core: 2. Of those that a mesh axis runs over, the one named last changes fastest.
Arguments:
- right_sides: bfloat16 [32, 131072], P(None, ('slab', 'leaf')), may hold values from -6 to 6
- left_sides: bfloat16 [32, 131072], P(None, ('slab', 'leaf')), may hold values from -6 to 6
- near_blocks: bfloat16 [1024, 8, 128, 128], P(('slab', 'leaf')), may hold values from -0.1875 to 0.1875
- near_columns: int32 [1024, 8], P(('slab', 'leaf')), may hold values from 0 to 1023, as said below
- cluster_points: int32 [1024], P(('slab', 'leaf')), may hold values from 64 to 128, as said below
- leaf_basis: bfloat16 [1024, 64, 128], P(('slab', 'leaf')), may hold values from -0.5 to 0.5
- transfer: float32 [1024, 64, 128], P(('slab', 'leaf')), may hold values from -0.625 to 0.625
- far_parents: int32 [32, 24], P(('slab', 'leaf')), may hold values from 0 to 31, as said below
- far_count: int32 [32], P(('slab', 'leaf')), may hold values from 12 to 24, as said below
- coupling: float32 [32, 24, 128, 128], P(('slab', 'leaf')), may hold values from -0.375 to 0.375
- slab_transfer: float32 [32, 128, 128], P(('slab', 'leaf')), may hold values from -0.75 to 0.75
- apex_coupling: float32 [4, 4, 128, 128], replicated, may hold values from -0.75 to 0.75
Outputs:
- product: float32 [32, 131072], P(None, ('slab', 'leaf'))
- adjoint_product: float32 [32, 131072], P(None, ('slab', 'leaf'))
Inputs may be any that keep to these rules, and one draw needn't show every extreme that they name: `near_columns`: row i holds 8 different clusters, i among them, all inside the window of 9 consecutive clusters centred on i, moved inward where it would pass an end of 0 to 1023. `cluster_points`: some cluster has exactly 128 points and some exactly 64. `far_parents`: row p holds 24 different parents, none equal to p; only the first far_count[p] are used. `far_count`: some parent uses all 24 slots and some exactly 12.
All inputs are finite; a program needn't handle non-finite values.
Results may differ from a plain program's by a relative error of at most 0.0024.
Values may be sent and summed in bfloat16 or wider, within the bound.
A program may use at most 128 MiB of HBM per device.

v0:
```python
import jax
import jax.numpy as jnp
from jax import lax
from jax.sharding import PartitionSpec as P

B = 128
HW = 4


def extended_2(value, sides, width):
    for axis, dim in sides:
        size, length = (lax.axis_size(axis), value.shape[dim])
        up = [(i, (i + 1) % size) for i in range(size - 1)]
        down = [(j, i) for i, j in up]
        last = lax.slice_in_dim(value, length - width, length, axis=dim)
        first = lax.slice_in_dim(value, 0, width, axis=dim)
        before = lax.ppermute(last, axis, up)
        after = lax.ppermute(first, axis, down)
        value = jnp.concatenate([before, value, after], axis=dim)
    return value


def passed_along(block, axis, distance):
    devices = range(lax.axis_size(axis))
    route = [(i - distance, i) for i in devices if i - distance in devices]
    return lax.ppermute(block, axis, route)


def shards(
    right_sides,
    left_sides,
    near_blocks,
    near_columns,
    cluster_points,
    leaf_basis,
    transfer,
    far_parents,
    far_count,
    coupling,
    slab_transfer,
    apex_coupling,
):
    uppermost_level = lax.Precision.HIGHEST
    rhs_count = right_sides.shape[0]
    clusters = near_blocks.shape[0]
    device = lax.axis_index(("slab", "leaf"))
    devices_all = lax.axis_size(("slab", "leaf"))
    slab_index = lax.axis_index("slab")
    slab_count = lax.axis_size("slab")
    point_mask = jnp.arange(B, dtype=jnp.int32)[None, :] < cluster_points[:, None]
    zero_bf = jnp.zeros((), jnp.bfloat16)
    masked_right = jnp.where(point_mask[None], right_sides.reshape(rhs_count, clusters, B), zero_bf)
    masked_left = jnp.where(point_mask[None], left_sides.reshape(rhs_count, clusters, B), zero_bf)
    extended = extended_2(
        masked_right.reshape(rhs_count, clusters * B), ((("slab", "leaf"), 1),), HW * B
    )
    extended = extended.reshape(rhs_count, clusters + 2 * HW, B)
    offsets = near_columns - (device * clusters - HW)
    picked = jnp.take(extended, offsets, axis=1)
    near_out = jnp.einsum("csab,rcsb->rca", near_blocks, picked, preferred_element_type=jnp.float32)
    contrib = jnp.einsum(
        "csab,rca->csrb", near_blocks, masked_left, preferred_element_type=jnp.float32
    )
    collected = jax.ops.segment_sum(
        contrib.reshape(-1, rhs_count, B), offsets.reshape(-1), num_segments=clusters + 2 * HW
    )
    from_next = passed_along(collected[:HW].astype(jnp.bfloat16), ("slab", "leaf"), -1).astype(
        jnp.float32
    )
    from_prev = passed_along(
        collected[clusters + HW :].astype(jnp.bfloat16), ("slab", "leaf"), 1
    ).astype(jnp.float32)
    middle = collected[HW : clusters + HW]
    middle = middle.at[clusters - HW :].add(from_next).at[:HW].add(from_prev)
    near_back = jnp.transpose(middle, (1, 0, 2))
    leaf_right = jnp.einsum(
        "ckb,rcb->ckr", leaf_basis, masked_right, preferred_element_type=jnp.float32
    )
    leaf_left = jnp.einsum(
        "ckb,rcb->ckr", leaf_basis, masked_left, preferred_element_type=jnp.float32
    )
    parent_right = jnp.einsum("ckq,ckr->qr", transfer, leaf_right, precision=uppermost_level)
    parent_left = jnp.einsum("ckq,ckr->qr", transfer, leaf_left, precision=uppermost_level)
    targets = far_parents[0]
    live_slots = jnp.arange(targets.shape[0], dtype=jnp.int32) < far_count[0]
    couple = coupling[0]
    piece = lax.all_gather(parent_right[None], ("slab", "leaf"), axis=0, tiled=True)
    owners = jnp.arange(piece.shape[0], dtype=jnp.int32)
    select = ((targets[:, None] == owners[None, :]) & live_slots[:, None]).astype(jnp.float32)
    chosen = jnp.einsum("fn,nqr->fqr", select, piece, precision=uppermost_level)
    far_right = jnp.einsum("fab,fbr->ar", couple, chosen, precision=uppermost_level)
    outward = jnp.einsum("fab,ar->fbr", couple, parent_left, precision=uppermost_level)
    routing = (
        (targets[:, None] == jnp.arange(devices_all, dtype=jnp.int32)[None, :])
        & live_slots[:, None]
    ).astype(jnp.float32)
    spread = jnp.einsum("fp,fbr->pbr", routing, outward, precision=uppermost_level)
    arrived = lax.all_to_all(spread, ("slab", "leaf"), split_axis=0, concat_axis=0, tiled=True)
    far_left = jnp.sum(arrived, axis=0)
    lift = slab_transfer[0]
    slab_share = jnp.stack(
        [
            jnp.einsum("qt,qr->tr", lift, parent_right, precision=uppermost_level),
            jnp.einsum("qt,qr->tr", lift, parent_left, precision=uppermost_level),
        ]
    )
    within = lax.psum(slab_share, "leaf")
    slab_sum_totals = lax.all_gather(within[None], "slab", axis=0, tiled=True)
    remaining_slabs = (jnp.arange(slab_count, dtype=jnp.int32) != slab_index).astype(jnp.float32)
    row_block_list = lax.dynamic_index_in_dim(apex_coupling, slab_index, 0, keepdims=False)
    column_blocks = lax.dynamic_index_in_dim(apex_coupling, slab_index, 1, keepdims=False)
    apex_right = jnp.einsum(
        "j,jiv,jvq->iq",
        remaining_slabs,
        row_block_list,
        slab_sum_totals[:, 0],
        precision=uppermost_level,
    )
    apex_left = jnp.einsum(
        "s,sab,sar->br",
        remaining_slabs,
        column_blocks,
        slab_sum_totals[:, 1],
        precision=uppermost_level,
    )
    hat_right = far_right + jnp.einsum("qt,tr->qr", lift, apex_right, precision=uppermost_level)
    hat_left = far_left + jnp.einsum("qt,tr->qr", lift, apex_left, precision=uppermost_level)
    down_right = jnp.einsum("ckq,qr->ckr", transfer, hat_right, precision=uppermost_level).astype(
        jnp.bfloat16
    )
    down_left = jnp.einsum("ckq,qr->ckr", transfer, hat_left, precision=uppermost_level).astype(
        jnp.bfloat16
    )
    far_out = jnp.einsum("ckb,ckr->rcb", leaf_basis, down_right, preferred_element_type=jnp.float32)
    far_back = jnp.einsum("ckb,ckr->rcb", leaf_basis, down_left, preferred_element_type=jnp.float32)
    zero_wide = jnp.zeros((), jnp.float32)
    product = jnp.where(point_mask[None], near_out + far_out, zero_wide).reshape(
        rhs_count, clusters * B
    )
    adjoint_product = jnp.where(point_mask[None], near_back + far_back, zero_wide).reshape(
        rhs_count, clusters * B
    )
    return (product, adjoint_product)


def solution(mesh):
    return jax.shard_map(
        shards,
        mesh=mesh,
        in_specs=(
            P(None, ("slab", "leaf")),
            P(None, ("slab", "leaf")),
            P(("slab", "leaf"), None, None, None),
            P(("slab", "leaf"), None),
            P(("slab", "leaf")),
            P(("slab", "leaf"), None, None),
            P(("slab", "leaf"), None, None),
            P(("slab", "leaf"), None),
            P(("slab", "leaf")),
            P(("slab", "leaf"), None, None, None),
            P(("slab", "leaf"), None, None),
            P(),
        ),
        out_specs=(P(None, ("slab", "leaf")), P(None, ("slab", "leaf"))),
        check_vma=False,
    )
```

profile of v0, /device:TPU:0, one launch (start us, length us, event | category | flops | bytes accessed | tf_op | source)
XLA Modules:
  0.0 178.2 jit_solution(13958339036343607816)
XLA Ops:
  0.7 0.8 compare_and_fusion
  1.5 0.1 reshape.132
  1.6 0.7 iota_compare_fusion
  2.4 6.7 %fusion.31 = f32[32,32,8,128]{3,1,2,0:T(8,128)} fusion(bf16[32,8,128,128]{3,2,1,0:T(8,128)(2,1)} %param.18, pred[32,128]{1,0:T(8,128)(4,1)S(1)} %iota_compare_fusion, bf16[32,4096]{1,0:T(8,128)(2,1)} %param.17), kind=kOutput, calls=%fused_computation.45 | convolution fusion | flops 268566528 | bytes 12849152 | tf_op jit(solution)/shard_map/csab,rca->csrb/dot_general | solution.py:61
  9.1 22.6 %scatter_fusion = f32[40,32,128]{2,1,0:T(8,128)S(1)} fusion(f32[40,32,128]{2,1,0:T(8,128)S(1)} %broadcast_in_dim.78, s32[256]{0:T(256)S(1)} %reshape.132, f32[256,32,128]{2,1,0:T(8,128)} %bitcast.168), kind=kCustom, calls=%fused_computation.1 | custom fusion | flops 1048576 | bytes 12583936 | tf_op jit(solution)/shard_map/scatter-add | solution.py:64
  31.8 0.6 fusion.70
  32.4 1.3 collective-permute-start.2
  33.7 3.7 %collective-permute-start.3 = (bf16[4,32,128]{2,1,0:T(8,128)(2,1)}, bf16[4,32,128]{2,1,0:T(8,128)(2,1)}, u32[]{:S(2)}, u32[]{:S(2)}) collective-permute-start(bf16[4,32,128]{2,1,0:T(8,128)(2,1)} %get-tuple-element.28), channel_id=1, source_target_pairs={{0,1},{1,2},{2,3},{3,4},{4,5},{5,6},{6,7},{7,8},{8,9},{9,10},{10,1... | collective-permute-start | bytes 98312 | tf_op jit(solution)/shard_map/ppermute | solution.py:26
  37.4 1.4 convolution_bitcast_fusion
  39.5 0.7 fusion.73
  40.3 0.9 fusion.15
  41.2 0.6 fusion.27
  41.9 1.1 copy.48
  43.0 10.2 %all-to-all-start = ((f32[32,128,32]{1,2,0:T(8,128)}), f32[32,128,32]{1,2,0:T(8,128)}, u32[]{:S(2)}, u32[]{:S(2)}) async-start(f32[32,128,32]{1,2,0:T(8,128)} %copy.48), calls=%async_computation | async-start | bytes 1048576 | tf_op jit(solution)/shard_map/all_to_all | solution.py:98
  53.3 1.0 broadcast_select_fusion
  54.3 0.6 fusion.71
  54.9 2.7 %collective-permute-start = (bf16[32,512]{1,0:T(8,128)(2,1)}, bf16[32,512]{1,0:T(8,128)(2,1)}, u32[]{:S(2)}, u32[]{:S(2)}) collective-permute-start(bf16[32,512]{1,0:T(8,128)(2,1)} %get-tuple-element.30), channel_id=1, source_target_pairs={{0,1},{1,2},{2,3},{3,4},{4,5},{5,6},{6,7},{7,8},{8,9},{9,10},{10,1... | collective-permute-start | bytes 98312 | tf_op jit(solution)/shard_map/ppermute | solution.py:17
  57.6 1.3 collective-permute-start.1
  58.9 2.3 %convolution_bitcast_fusion.1 = f32[32,64,32]{1,2,0:T(8,128)} fusion(bf16[32,64,128]{2,1,0:T(8,128)(2,1)} %param.21, pred[32,128]{1,0:T(8,128)(4,1)S(1)} %iota_compare_fusion, bf16[32,4096]{1,0:T(8,128)(2,1)} %param.16), kind=kOutput, calls=%fused_computation.12 | convolution fusion | flops 16908288 | bytes 1052672 | tf_op jit(solution)/shard_map/ckb,rcb->ckr/dot_general | solution.py:76
  61.2 1.0 convolution_bitcast_fusion.5
  62.2 1.8 %fusion.72 = f32[32,128,1]{1,0,2:T(8,128)S(1)} fusion(f32[32,64,32]{1,2,0:T(8,128)} %convolution_bitcast_fusion.1, f32[32,64,128]{2,1,0:T(8,128)S(1)} %copy-done.1), kind=kOutput, calls=%fused_computation.97 | convolution fusion | flops 100663296 | bytes 1327104 | tf_op jit(solution)/shard_map/ckq,ckr->qr/dot_general | solution.py:82
  64.0 0.6 copy-done.9
  64.6 1.0 convolution_bitcast_fusion.6
  65.6 0.6 maximum_bitcast_fusion.1
  66.2 31.6 %psum.7 = f32[1,2,128,32]{2,3,1,0:T(8,128)} all-reduce(f32[1,2,128,32]{2,3,1,0:T(8,128)} %maximum_bitcast_fusion.1), channel_id=1, replica_groups=mesh['slab'=4,'leaf'=8] {'leaf'}, use_global_device_ids=true, to_apply=%region_0.1 | all-reduce | flops 8192 | bytes 65536 | tf_op jit(solution)/shard_map/psum | solution.py:107
  97.8 10.0 %all_gather.7 = f32[4,2,128,32]{2,3,1,0:T(8,128)} all-gather(f32[1,2,128,32]{2,3,1,0:T(8,128)} %psum.7), channel_id=1, replica_groups=mesh['slab'=4,'leaf'=8] {'slab'}, dimensions={0}, use_global_device_ids=true | all-gather | bytes 163840 | tf_op jit(solution)/shard_map/all_gather | solution.py:108
  107.8 1.8 %convolution_bitcast_fusion.3 = f32[128,32]{0,1:T(8,128)} fusion(f32[4,4,128,128]{3,2,1,0:T(8,128)} %param.27, s32[]{:T(128)S(6)} %select_n.42, f32[4,2,128,32]{2,3,1,0:T(8,128)} %all_gather.7, f32[4]{0:T(128)S(1)} %compare_convert_fusion), kind=kOutput, calls=%fused_computation.28 | convolution fusion | flops 25182208 | bytes 344084 | tf_op jit(solution)/shard_map/s,sab,sar->br/dot_general | solution.py:119
  109.6 1.4 convolution_bitcast_fusion.4
  111.0 39.0 %all-gather = f32[4096,32]{0,1:T(8,128)S(1)} all-gather(f32[128,32]{0,1:T(8,128)} %bitcast.174), channel_id=2, replica_groups=mesh['slab'=4,'leaf'=8] {'slab','leaf'}, dimensions={0}, use_global_device_ids=true | all-gather | bytes 540672 | tf_op jit(solution)/shard_map/all_gather | solution.py:87
  150.0 0.1 copy.58
  150.1 1.0 fusion.58
  151.2 1.6 fusion.20
  152.8 0.2 fusion.25
  153.0 3.6 %fusion.18 = bf16[32,64,32]{1,2,0:T(8,128)(2,1)} fusion(f32[32,128,1]{1,0,2:T(8,128)S(1)} %fusion.25, f32[32,64,128]{2,1,0:T(8,128)S(1)} %copy-done.1), kind=kOutput, calls=%fused_computation.22 | convolution fusion | flops 100728832 | bytes 1196032 | tf_op jit(solution)/shard_map/ckq,qr->ckr/dot_general | solution.py:128
  156.8 0.8 slice.86
  157.6 0.1 copy.38
  157.7 0.8 copy_bitcast_fusion.2
  158.6 2.2 %gather_fusion = bf16[256,32,128]{2,1,0:T(8,128)(2,1)} fusion(bf16[32,40,128]{2,0,1:T(8,128)(2,1)S(1)} %copy_bitcast_fusion.2, s32[1024]{0:T(1024)S(1)} %pad_clamp_fusion), kind=kCustom, calls=%fused_computation | custom fusion | bytes 4195328 | tf_op jit(solution)/shard_map/jit(_take)/gather | solution.py:59
  160.8 1.4 fusion.44
  162.2 6.9 %fusion.8 = f32[32,32,128]{2,1,0:T(8,128)S(1)} fusion(bf16[32,8,128,128]{3,2,1,0:T(8,128)(2,1)} %param.18, bf16[32,8,32,128]{3,2,1,0:T(8,128)(2,1)} %bitcast.169, pred[32,8]{1,0:T(8,128)(4,1)S(1)} %copy.38), kind=kOutput, calls=%fused_computation.10 | convolution fusion | flops 269484032 | bytes 11010304 | tf_op jit(solution)/shard_map/csab,rcsb->rca/dot_general | solution.py:60
  169.2 0.3 fusion.14
  169.5 0.8 copy.76
  170.3 1.5 fusion.43
  171.8 1.1 reduce_sum.9
  172.9 0.2 fusion.24
  173.1 2.9 %fusion.19 = bf16[32,64,32]{1,2,0:T(8,128)(2,1)S(1)} fusion(f32[128,32,1]{0,1,2:T(8,128)S(1)} %fusion.24, f32[32,64,128]{2,1,0:T(8,128)S(1)} %copy-done.2), kind=kOutput, calls=%fused_computation.23 | convolution fusion | flops 100728832 | bytes 1196032 | tf_op jit(solution)/shard_map/ckq,qr->ckr/dot_general | solution.py:131
  176.0 1.3 fusion.12
  177.4 0.8 copy.75
  (43 shorter events, 0.6 us)
Async XLA Ops:
  0.6 39.6 %copy-start = (f32[1,24,128,128]{3,2,1,0:T(8,128)S(1)}, f32[1,24,128,128]{3,2,1,0:T(8,128)}, u32[]{:S(2)}) copy-start(f32[1,24,128,128]{3,2,1,0:T(8,128)} %param.25) | copy-start | bytes 4718596
  9.1 28.3 %copy-start.4 = (bf16[32,4096]{1,0:T(8,128)(2,1)S(1)}, bf16[32,4096]{1,0:T(8,128)(2,1)}, u32[]{:S(2)}) copy-start(bf16[32,4096]{1,0:T(8,128)(2,1)} %param.17) | copy-start | bytes 786436
  31.7 7.8 %copy-start.1 = (f32[32,64,128]{2,1,0:T(8,128)S(1)}, f32[32,64,128]{2,1,0:T(8,128)}, u32[]{:S(2)}) copy-start(f32[32,64,128]{2,1,0:T(8,128)} %param.22) | copy-start | bytes 3145732
  32.4 128.4 %collective-permute-start.2 = (bf16[4,32,128]{2,1,0:T(8,128)(2,1)}, bf16[4,32,128]{2,1,0:T(8,128)(2,1)}, u32[]{:S(2)}, u32[]{:S(2)}) collective-permute-start(bf16[4,32,128]{2,1,0:T(8,128)(2,1)} %get-tuple-element.29), channel_id=1, source_target_pairs={{1,0},{2,1},{3,2},{4,3},{5,4},{6,5},{7,6},{8,7},{9,8},{10,9},{11,1... | collective-permute-start | bytes 98312 | tf_op jit(solution)/shard_map/ppermute | solution.py:26
  33.7 136.6 %collective-permute-start.3 = (bf16[4,32,128]{2,1,0:T(8,128)(2,1)}, bf16[4,32,128]{2,1,0:T(8,128)(2,1)}, u32[]{:S(2)}, u32[]{:S(2)}) collective-permute-start(bf16[4,32,128]{2,1,0:T(8,128)(2,1)} %get-tuple-element.28), channel_id=1, source_target_pairs={{0,1},{1,2},{2,3},{3,4},{4,5},{5,6},{6,7},{7,8},{8,9},{9,10},{10,1... | collective-permute-start | bytes 98312 | tf_op jit(solution)/shard_map/ppermute | solution.py:26
  38.8 2.4 %copy-start.11 = (s32[1,24]{1,0:T(1,128)S(1)}, s32[1,24]{1,0:T(1,128)}, u32[]{:S(2)}) copy-start(s32[1,24]{1,0:T(1,128)} %param.23) | copy-start | bytes 292
  39.5 2.4 %copy-start.12 = (pred[24]{0:T(512)(128)(4,1)}, pred[24]{0:T(512)(128)(4,1)S(1)}, u32[]{:S(2)}) copy-start(pred[24]{0:T(512)(128)(4,1)S(1)} %iota_compare_fusion.2) | copy-start | bytes 76
  40.2 2.7 %copy-start.8 = (f32[32,128,1]{1,0,2:T(8,128)}, f32[32,128,1]{1,0,2:T(8,128)S(1)}, u32[]{:S(2)}) copy-start(f32[32,128,1]{1,0,2:T(8,128)S(1)} %fusion.73) | copy-start | bytes 49156
  40.3 12.9 %copy-start.13 = (s32[32]{0:T(128)S(1)}, s32[32]{0:T(128)}, u32[]{:S(2)}) copy-start(s32[32]{0:T(128)} %param.20) | copy-start | bytes 388
  43.0 128.8 %all-to-all-start = ((f32[32,128,32]{1,2,0:T(8,128)}), f32[32,128,32]{1,2,0:T(8,128)}, u32[]{:S(2)}, u32[]{:S(2)}) async-start(f32[32,128,32]{1,2,0:T(8,128)} %copy.48), calls=%async_computation | async-start | bytes 1048576 | tf_op jit(solution)/shard_map/all_to_all | solution.py:98
  54.9 102.8 %collective-permute-start = (bf16[32,512]{1,0:T(8,128)(2,1)}, bf16[32,512]{1,0:T(8,128)(2,1)}, u32[]{:S(2)}, u32[]{:S(2)}) collective-permute-start(bf16[32,512]{1,0:T(8,128)(2,1)} %get-tuple-element.30), channel_id=1, source_target_pairs={{0,1},{1,2},{2,3},{3,4},{4,5},{5,6},{6,7},{7,8},{8,9},{9,10},{10,1... | collective-permute-start | bytes 98312 | tf_op jit(solution)/shard_map/ppermute | solution.py:17
  57.6 100.2 %collective-permute-start.1 = (bf16[32,512]{1,0:T(8,128)(2,1)}, bf16[32,512]{1,0:T(8,128)(2,1)}, u32[]{:S(2)}, u32[]{:S(2)}) collective-permute-start(bf16[32,512]{1,0:T(8,128)(2,1)} %get-tuple-element.31), channel_id=1, source_target_pairs={{1,0},{2,1},{3,2},{4,3},{5,4},{6,5},{7,6},{8,7},{9,8},{10,9},{11,1... | collective-permute-start | bytes 98312 | tf_op jit(solution)/shard_map/ppermute | solution.py:18
  64.0 0.6 copy-start.9
  150.0 2.8 %copy-start.5 = (f32[1,128,128]{2,1,0:T(8,128)S(1)}, f32[1,128,128]{2,1,0:T(8,128)}, u32[]{:S(2)}) copy-start(f32[1,128,128]{2,1,0:T(8,128)} %param.26) | copy-start | bytes 196612
  162.2 7.0 %copy-start.3 = (bf16[32,64,128]{2,1,0:T(8,128)(2,1)S(1)}, bf16[32,64,128]{2,1,0:T(8,128)(2,1)}, u32[]{:S(2)}) copy-start(bf16[32,64,128]{2,1,0:T(8,128)(2,1)} %param.21) | copy-start | bytes 1572868
  162.2 7.0 %copy-start.7 = (bf16[32,64,32]{1,2,0:T(8,128)(2,1)S(1)}, bf16[32,64,32]{1,2,0:T(8,128)(2,1)}, u32[]{:S(2)}) copy-start(bf16[32,64,32]{1,2,0:T(8,128)(2,1)} %fusion.18) | copy-start | bytes 393220
  169.2 3.7 %copy-start.6 = (f32[1,128,128]{2,1,0:T(8,128)S(1)}, f32[1,128,128]{2,1,0:T(8,128)}, u32[]{:S(2)}) copy-start(f32[1,128,128]{2,1,0:T(8,128)} %param.26) | copy-start | bytes 196612
  169.2 3.7 %copy-start.10 = (f32[128,32]{0,1:T(8,128)S(1)}, f32[128,32]{0,1:T(8,128)}, u32[]{:S(2)}) copy-start(f32[128,32]{0,1:T(8,128)} %convolution_bitcast_fusion.3) | copy-start | bytes 49156
  169.2 3.9 %copy-start.2 = (f32[32,64,128]{2,1,0:T(8,128)S(1)}, f32[32,64,128]{2,1,0:T(8,128)}, u32[]{:S(2)}) copy-start(f32[32,64,128]{2,1,0:T(8,128)} %param.22) | copy-start | bytes 3145732
where the time goes:
time: 180 us; the launch traced here: 178 us
  blocking collectives  80.6 us (45%)
  matrix products  37.8 us (21%)
  other arithmetic  30.6 us (17%)
  starting transfers between devices  19.1 us (11%)
  local copies, waits for them, and re-layouts  8.43 us (5%)
    all_gather x1, blocking collectives, shards(): lax.all_gather(parent_right[None], ('slab', 'leaf'), axis=0, tiled=True)  39 us
    psum x1, blocking collectives, shards(): within = lax.psum(slab_share, 'leaf')  31.6 us
    scatter-add x1, other arithmetic, shards(): jax.ops.segment_sum(contrib.reshape(-1, rhs_count, B), offsets.reshape(-1...  22.6 us
    all_to_all x1, starting transfers between devices, shards(): lax.all_to_all(spread, ('slab', 'leaf'), split_axis=0, concat_axis=0, til...  10.2 us
    all_gather x1, blocking collectives, shards(): slab_sum_totals = lax.all_gather(within[None], 'slab', axis=0, tiled=True)  9.96 us
    dot_general x1, matrix products, shards(): jnp.einsum('csab,rcsb->rca', near_blocks, picked, preferred_element_type=...  6.94 us
    dot_general x1, matrix products, shards(): jnp.einsum('csab,rca->csrb', near_blocks, masked_left, preferred_element_...  6.65 us
    ppermute x2, starting transfers between devices, passed_along(): return lax.ppermute(block, axis, route)  4.93 us
  transfers between devices with their start and end apart: 5, of which 0 were waited for; matrix products, arithmetic and copies ran while one was open for 21% of the time, Pallas kernels for 0%

commit v1 on v0

--- a/solution.py
+++ b/solution.py
@@ -104,7 +104,7 @@
             jnp.einsum("qt,qr->tr", lift, parent_left, precision=uppermost_level),
         ]
     )
-    within = lax.psum(slab_share, "leaf")
+    within = jnp.sum(lax.all_gather(slab_share, "leaf"), axis=0)
     slab_sum_totals = lax.all_gather(within[None], "slab", axis=0, tiled=True)
     remaining_slabs = (jnp.arange(slab_count, dtype=jnp.int32) != slab_index).astype(jnp.float32)
     row_block_list = lax.dynamic_index_in_dim(apex_coupling, slab_index, 0, keepdims=False)

time: 180 us -> 170 us (0.944)
  blocking collectives: 80.6 us -> 70 us
    psum x1 -> x0, blocking collectives: 31.6 us -> none  [shards(): within = lax.psum(slab_share, 'leaf')]
    all_gather x0 -> x1, blocking collectives: none -> 17.2 us  [shards(): within = jnp.sum(lax.all_gather(slab_share, 'leaf'), axis=0)]
    all_gather x1, blocking collectives: 9.96 us -> 12.6 us  [shards(): slab_sum_totals = lax.all_gather(within[None], 'slab', axis=0, tiled=True)]
  transfers between devices with their start and end apart: 5 -> 5, of which waited for: 0 -> 0; matrix products, arithmetic and copies ran while one was open for 21% -> 23% of each run, Pallas kernels for 0% -> 0%
where the time goes in v1:
time: 170 us; the launch traced here: 169 us
  blocking collectives  70 us (41%)
  matrix products  37.8 us (22%)
  other arithmetic  31.6 us (19%)
  starting transfers between devices  19.1 us (11%)
  local copies, waits for them, and re-layouts  8.43 us (5%)
  between operations  1.71 us (1%)
    all_gather x1, blocking collectives, shards(): lax.all_gather(parent_right[None], ('slab', 'leaf'), axis=0, tiled=True)  40.3 us
    scatter-add x1, other arithmetic, shards(): jax.ops.segment_sum(contrib.reshape(-1, rhs_count, B), offsets.reshape(-1...  22.6 us
    all_gather x1, blocking collectives, shards(): within = jnp.sum(lax.all_gather(slab_share, 'leaf'), axis=0)  17.2 us
    all_gather x1, blocking collectives, shards(): slab_sum_totals = lax.all_gather(within[None], 'slab', axis=0, tiled=True)  12.6 us
    all_to_all x1, starting transfers between devices, shards(): lax.all_to_all(spread, ('slab', 'leaf'), split_axis=0, concat_axis=0, til...  10.2 us
    dot_general x1, matrix products, shards(): jnp.einsum('csab,rcsb->rca', near_blocks, picked, preferred_element_type=...  6.94 us
    dot_general x1, matrix products, shards(): jnp.einsum('csab,rca->csrb', near_blocks, masked_left, preferred_element_...  6.65 us
    ppermute x2, starting transfers between devices, passed_along(): return lax.ppermute(block, axis, route)  4.93 us
  transfers between devices with their start and end apart: 5, of which 0 were waited for; matrix products, arithmetic and copies ran while one was open for 23% of the time, Pallas kernels for 0%

profile of v1, /device:TPU:0, one launch (start us, length us, event | category | flops | bytes accessed | tf_op | source)
XLA Modules:
  0.0 168.6 jit_solution(3837336940379929815)
XLA Ops:
  0.7 0.8 compare_and_fusion
  1.5 0.1 reshape.132
  1.6 0.7 iota_compare_fusion
  2.4 6.7 %fusion.31 = f32[32,32,8,128]{3,1,2,0:T(8,128)} fusion(bf16[32,8,128,128]{3,2,1,0:T(8,128)(2,1)} %param.18, pred[32,128]{1,0:T(8,128)(4,1)S(1)} %iota_compare_fusion, bf16[32,4096]{1,0:T(8,128)(2,1)} %param.17), kind=kOutput, calls=%fused_computation.45 | convolution fusion | flops 268566528 | bytes 12849152 | tf_op jit(solution)/shard_map/csab,rca->csrb/dot_general | solution.py:61
  9.1 22.6 %scatter_fusion = f32[40,32,128]{2,1,0:T(8,128)S(1)} fusion(f32[40,32,128]{2,1,0:T(8,128)S(1)} %broadcast_in_dim.78, s32[256]{0:T(256)S(1)} %reshape.132, f32[256,32,128]{2,1,0:T(8,128)} %bitcast.168), kind=kCustom, calls=%fused_computation.1 | custom fusion | flops 1048576 | bytes 12583936 | tf_op jit(solution)/shard_map/scatter-add | solution.py:64
  31.8 0.6 fusion.70
  32.4 1.3 collective-permute-start.2
  33.7 3.7 %collective-permute-start.3 = (bf16[4,32,128]{2,1,0:T(8,128)(2,1)}, bf16[4,32,128]{2,1,0:T(8,128)(2,1)}, u32[]{:S(2)}, u32[]{:S(2)}) collective-permute-start(bf16[4,32,128]{2,1,0:T(8,128)(2,1)} %get-tuple-element.28), channel_id=1, source_target_pairs={{0,1},{1,2},{2,3},{3,4},{4,5},{5,6},{6,7},{7,8},{8,9},{9,10},{10,1... | collective-permute-start | bytes 98312 | tf_op jit(solution)/shard_map/ppermute | solution.py:26
  37.4 1.4 convolution_bitcast_fusion
  39.5 0.7 fusion.73
  40.3 0.9 fusion.15
  41.2 0.6 fusion.27
  41.9 1.1 copy.47
  43.0 10.2 %all-to-all-start = ((f32[32,128,32]{1,2,0:T(8,128)}), f32[32,128,32]{1,2,0:T(8,128)}, u32[]{:S(2)}, u32[]{:S(2)}) async-start(f32[32,128,32]{1,2,0:T(8,128)} %copy.47), calls=%async_computation | async-start | bytes 1048576 | tf_op jit(solution)/shard_map/all_to_all | solution.py:98
  53.3 1.0 broadcast_select_fusion
  54.3 0.6 fusion.71
  54.9 2.7 %collective-permute-start = (bf16[32,512]{1,0:T(8,128)(2,1)}, bf16[32,512]{1,0:T(8,128)(2,1)}, u32[]{:S(2)}, u32[]{:S(2)}) collective-permute-start(bf16[32,512]{1,0:T(8,128)(2,1)} %get-tuple-element.30), channel_id=1, source_target_pairs={{0,1},{1,2},{2,3},{3,4},{4,5},{5,6},{6,7},{7,8},{8,9},{9,10},{10,1... | collective-permute-start | bytes 98312 | tf_op jit(solution)/shard_map/ppermute | solution.py:17
  57.6 1.3 collective-permute-start.1
  58.9 2.3 %convolution_bitcast_fusion.1 = f32[32,64,32]{1,2,0:T(8,128)} fusion(bf16[32,64,128]{2,1,0:T(8,128)(2,1)} %param.21, pred[32,128]{1,0:T(8,128)(4,1)S(1)} %iota_compare_fusion, bf16[32,4096]{1,0:T(8,128)(2,1)} %param.16), kind=kOutput, calls=%fused_computation.12 | convolution fusion | flops 16908288 | bytes 1052672 | tf_op jit(solution)/shard_map/ckb,rcb->ckr/dot_general | solution.py:76
  61.2 1.0 convolution_bitcast_fusion.5
  62.2 1.8 %fusion.72 = f32[32,128,1]{1,0,2:T(8,128)S(1)} fusion(f32[32,64,32]{1,2,0:T(8,128)} %convolution_bitcast_fusion.1, f32[32,64,128]{2,1,0:T(8,128)S(1)} %copy-done.1), kind=kOutput, calls=%fused_computation.97 | convolution fusion | flops 100663296 | bytes 1327104 | tf_op jit(solution)/shard_map/ckq,ckr->qr/dot_general | solution.py:82
  64.0 0.6 copy-done.9
  64.6 1.0 convolution_bitcast_fusion.6
  65.6 17.2 %all-gather.1 = f32[16,128,32]{1,2,0:T(8,128)} all-gather(f32[2,128,32]{1,2,0:T(8,128)S(1)} %pad_maximum_fusion), channel_id=3, replica_groups=mesh['slab'=4,'leaf'=8] {'leaf'}, dimensions={0}, use_global_device_ids=true | all-gather | bytes 294912 | tf_op jit(solution)/shard_map/all_gather | solution.py:107
  82.8 1.6 reduce_sum.18
  84.4 12.6 %all-gather.2 = f32[8,128,32]{1,2,0:T(8,128)} all-gather(f32[2,128,32]{1,2,0:T(8,128)} %reduce_sum.18), channel_id=4, replica_groups=mesh['slab'=4,'leaf'=8] {'slab'}, dimensions={0}, use_global_device_ids=true | all-gather | bytes 163840 | tf_op jit(solution)/shard_map/all_gather | solution.py:108
  97.0 1.8 %convolution_bitcast_fusion.3 = f32[128,32]{0,1:T(8,128)} fusion(f32[4,4,128,128]{3,2,1,0:T(8,128)} %param.27, s32[]{:T(128)S(6)} %select_n.42, f32[4,2,128,32]{2,3,1,0:T(8,128)} %bitcast.175, f32[4]{0:T(128)S(1)} %compare_convert_fusion), kind=kOutput, calls=%fused_computation.28 | convolution fusion | flops 25182208 | bytes 344084 | tf_op jit(solution)/shard_map/s,sab,sar->br/dot_general | solution.py:119
  98.8 1.3 convolution_bitcast_fusion.4
  100.2 40.3 %all-gather = f32[4096,32]{0,1:T(8,128)S(1)} all-gather(f32[128,32]{0,1:T(8,128)} %bitcast.177), channel_id=2, replica_groups=mesh['slab'=4,'leaf'=8] {'slab','leaf'}, dimensions={0}, use_global_device_ids=true | all-gather | bytes 540672 | tf_op jit(solution)/shard_map/all_gather | solution.py:87
  140.5 0.1 copy.57
  140.6 1.0 fusion.58
  141.6 1.6 fusion.20
  143.3 0.2 fusion.25
  143.5 3.6 %fusion.18 = bf16[32,64,32]{1,2,0:T(8,128)(2,1)} fusion(f32[32,128,1]{1,0,2:T(8,128)S(1)} %fusion.25, f32[32,64,128]{2,1,0:T(8,128)S(1)} %copy-done.1), kind=kOutput, calls=%fused_computation.22 | convolution fusion | flops 100728832 | bytes 1196032 | tf_op jit(solution)/shard_map/ckq,qr->ckr/dot_general | solution.py:128
  147.3 0.8 slice.86
  148.1 0.1 copy.37
  148.2 0.8 copy_bitcast_fusion.2
  149.0 2.2 %gather_fusion = bf16[256,32,128]{2,1,0:T(8,128)(2,1)} fusion(bf16[32,40,128]{2,0,1:T(8,128)(2,1)S(1)} %copy_bitcast_fusion.2, s32[1024]{0:T(1024)S(1)} %pad_clamp_fusion), kind=kCustom, calls=%fused_computation | custom fusion | bytes 4195328 | tf_op jit(solution)/shard_map/jit(_take)/gather | solution.py:59
  151.2 1.4 fusion.44
  152.6 6.9 %fusion.8 = f32[32,32,128]{2,1,0:T(8,128)S(1)} fusion(bf16[32,8,128,128]{3,2,1,0:T(8,128)(2,1)} %param.18, bf16[32,8,32,128]{3,2,1,0:T(8,128)(2,1)} %bitcast.169, pred[32,8]{1,0:T(8,128)(4,1)S(1)} %copy.37), kind=kOutput, calls=%fused_computation.10 | convolution fusion | flops 269484032 | bytes 11010304 | tf_op jit(solution)/shard_map/csab,rcsb->rca/dot_general | solution.py:60
  159.7 0.3 fusion.14
  159.9 0.8 copy.75
  160.8 1.5 fusion.43
  162.2 1.1 reduce_sum.19
  163.3 0.2 fusion.24
  163.6 2.9 %fusion.19 = bf16[32,64,32]{1,2,0:T(8,128)(2,1)S(1)} fusion(f32[128,32,1]{0,1,2:T(8,128)S(1)} %fusion.24, f32[32,64,128]{2,1,0:T(8,128)S(1)} %copy-done.2), kind=kOutput, calls=%fused_computation.23 | convolution fusion | flops 100728832 | bytes 1196032 | tf_op jit(solution)/shard_map/ckq,qr->ckr/dot_general | solution.py:131
  166.5 1.3 fusion.12
  167.8 0.8 copy.74
  (44 shorter events, 0.6 us)
Async XLA Ops:
  0.6 39.6 %copy-start = (f32[1,24,128,128]{3,2,1,0:T(8,128)S(1)}, f32[1,24,128,128]{3,2,1,0:T(8,128)}, u32[]{:S(2)}) copy-start(f32[1,24,128,128]{3,2,1,0:T(8,128)} %param.25) | copy-start | bytes 4718596
  9.1 28.3 %copy-start.4 = (bf16[32,4096]{1,0:T(8,128)(2,1)S(1)}, bf16[32,4096]{1,0:T(8,128)(2,1)}, u32[]{:S(2)}) copy-start(bf16[32,4096]{1,0:T(8,128)(2,1)} %param.17) | copy-start | bytes 786436
  31.7 7.8 %copy-start.1 = (f32[32,64,128]{2,1,0:T(8,128)S(1)}, f32[32,64,128]{2,1,0:T(8,128)}, u32[]{:S(2)}) copy-start(f32[32,64,128]{2,1,0:T(8,128)} %param.22) | copy-start | bytes 3145732
  32.4 118.8 %collective-permute-start.2 = (bf16[4,32,128]{2,1,0:T(8,128)(2,1)}, bf16[4,32,128]{2,1,0:T(8,128)(2,1)}, u32[]{:S(2)}, u32[]{:S(2)}) collective-permute-start(bf16[4,32,128]{2,1,0:T(8,128)(2,1)} %get-tuple-element.29), channel_id=1, source_target_pairs={{1,0},{2,1},{3,2},{4,3},{5,4},{6,5},{7,6},{8,7},{9,8},{10,9},{11,1... | collective-permute-start | bytes 98312 | tf_op jit(solution)/shard_map/ppermute | solution.py:26
  33.7 127.1 %collective-permute-start.3 = (bf16[4,32,128]{2,1,0:T(8,128)(2,1)}, bf16[4,32,128]{2,1,0:T(8,128)(2,1)}, u32[]{:S(2)}, u32[]{:S(2)}) collective-permute-start(bf16[4,32,128]{2,1,0:T(8,128)(2,1)} %get-tuple-element.28), channel_id=1, source_target_pairs={{0,1},{1,2},{2,3},{3,4},{4,5},{5,6},{6,7},{7,8},{8,9},{9,10},{10,1... | collective-permute-start | bytes 98312 | tf_op jit(solution)/shard_map/ppermute | solution.py:26
  38.8 2.4 %copy-start.11 = (s32[1,24]{1,0:T(1,128)S(1)}, s32[1,24]{1,0:T(1,128)}, u32[]{:S(2)}) copy-start(s32[1,24]{1,0:T(1,128)} %param.23) | copy-start | bytes 292
  39.5 2.4 %copy-start.12 = (pred[24]{0:T(512)(128)(4,1)}, pred[24]{0:T(512)(128)(4,1)S(1)}, u32[]{:S(2)}) copy-start(pred[24]{0:T(512)(128)(4,1)S(1)} %iota_compare_fusion.2) | copy-start | bytes 76
  40.2 2.7 %copy-start.8 = (f32[32,128,1]{1,0,2:T(8,128)}, f32[32,128,1]{1,0,2:T(8,128)S(1)}, u32[]{:S(2)}) copy-start(f32[32,128,1]{1,0,2:T(8,128)S(1)} %fusion.73) | copy-start | bytes 49156
  40.3 12.9 %copy-start.13 = (s32[32]{0:T(128)S(1)}, s32[32]{0:T(128)}, u32[]{:S(2)}) copy-start(s32[32]{0:T(128)} %param.20) | copy-start | bytes 388
  43.0 119.3 %all-to-all-start = ((f32[32,128,32]{1,2,0:T(8,128)}), f32[32,128,32]{1,2,0:T(8,128)}, u32[]{:S(2)}, u32[]{:S(2)}) async-start(f32[32,128,32]{1,2,0:T(8,128)} %copy.47), calls=%async_computation | async-start | bytes 1048576 | tf_op jit(solution)/shard_map/all_to_all | solution.py:98
  54.9 93.3 %collective-permute-start = (bf16[32,512]{1,0:T(8,128)(2,1)}, bf16[32,512]{1,0:T(8,128)(2,1)}, u32[]{:S(2)}, u32[]{:S(2)}) collective-permute-start(bf16[32,512]{1,0:T(8,128)(2,1)} %get-tuple-element.30), channel_id=1, source_target_pairs={{0,1},{1,2},{2,3},{3,4},{4,5},{5,6},{6,7},{7,8},{8,9},{9,10},{10,1... | collective-permute-start | bytes 98312 | tf_op jit(solution)/shard_map/ppermute | solution.py:17
  57.6 90.6 %collective-permute-start.1 = (bf16[32,512]{1,0:T(8,128)(2,1)}, bf16[32,512]{1,0:T(8,128)(2,1)}, u32[]{:S(2)}, u32[]{:S(2)}) collective-permute-start(bf16[32,512]{1,0:T(8,128)(2,1)} %get-tuple-element.31), channel_id=1, source_target_pairs={{1,0},{2,1},{3,2},{4,3},{5,4},{6,5},{7,6},{8,7},{9,8},{10,9},{11,1... | collective-permute-start | bytes 98312 | tf_op jit(solution)/shard_map/ppermute | solution.py:18
  64.0 0.6 copy-start.9
  140.5 2.8 %copy-start.5 = (f32[1,128,128]{2,1,0:T(8,128)S(1)}, f32[1,128,128]{2,1,0:T(8,128)}, u32[]{:S(2)}) copy-start(f32[1,128,128]{2,1,0:T(8,128)} %param.26) | copy-start | bytes 196612
  152.6 7.0 %copy-start.3 = (bf16[32,64,128]{2,1,0:T(8,128)(2,1)S(1)}, bf16[32,64,128]{2,1,0:T(8,128)(2,1)}, u32[]{:S(2)}) copy-start(bf16[32,64,128]{2,1,0:T(8,128)(2,1)} %param.21) | copy-start | bytes 1572868
  152.6 7.0 %copy-start.7 = (bf16[32,64,32]{1,2,0:T(8,128)(2,1)S(1)}, bf16[32,64,32]{1,2,0:T(8,128)(2,1)}, u32[]{:S(2)}) copy-start(bf16[32,64,32]{1,2,0:T(8,128)(2,1)} %fusion.18) | copy-start | bytes 393220
  159.6 3.7 %copy-start.6 = (f32[1,128,128]{2,1,0:T(8,128)S(1)}, f32[1,128,128]{2,1,0:T(8,128)}, u32[]{:S(2)}) copy-start(f32[1,128,128]{2,1,0:T(8,128)} %param.26) | copy-start | bytes 196612
  159.6 3.7 %copy-start.10 = (f32[128,32]{0,1:T(8,128)S(1)}, f32[128,32]{0,1:T(8,128)}, u32[]{:S(2)}) copy-start(f32[128,32]{0,1:T(8,128)} %convolution_bitcast_fusion.3) | copy-start | bytes 49156
  159.6 3.9 %copy-start.2 = (f32[32,64,128]{2,1,0:T(8,128)S(1)}, f32[32,64,128]{2,1,0:T(8,128)}, u32[]{:S(2)}) copy-start(f32[32,64,128]{2,1,0:T(8,128)} %param.22) | copy-start | bytes 3145732
